TPU v7x, 32 devices: a whole 2x2x4 slice. The times are simulated.
32 devices in a mesh: grp: 4 (over y, core), dev: 8 (over z, x).
Axes of the slice: x: 2, y: 2, z: 4, core: 2. Of those that a mesh axis runs over, the one named last changes fastest.
Arguments:
- visibilities: bfloat16 [16384, 2, 128], P(('grp', 'dev')), may hold values from -6 to 6
- owner: int32 [16384, 1], P(('grp', 'dev')), may hold values from 0 to 31; in each aligned block of 512 rows (0 to 511, 512 to 1023, ...) at most 32 rows name the same one
- tile_slot: int32 [16384], P(('grp', 'dev')), may hold values from 0 to 511
- kernel_index: int32 [16384, 2], P(('grp', 'dev')), may hold values from 0 to 31
- kernels: bfloat16 [2, 32, 64, 128], replicated, may hold values from -1 to 1
Outputs:
- image: float32 [2, 8192, 8192], P(None, ('grp', 'dev'))
Inputs may be any that keep to these rules, and one draw needn't show every extreme that they name: owner[r, 0] = g * 8 + d names group g and owner d; among the rows of one device no owner is named by more than 32 rows, a bound that some block reaches.
All inputs are finite; a program needn't handle non-finite values.
Results may differ from a plain program's by a relative error of at most 0.0029.
Values may be sent and summed in bfloat16 or wider, within the bound.
A program may use at most 128 MiB of HBM per device.

v0:
```python
import math

import jax
import jax.numpy as jnp
from jax import lax
from jax.sharding import PartitionSpec as P

GRID = 8192
TILE = 64
VIS = 128
QLEN = 128


def complex_product(pattern, left_re, left_im, right_re, right_im):

    def product(first, second):
        return jnp.einsum(pattern, first, second, precision=lax.Precision.HIGHEST)

    return (
        product(left_re, right_re) - product(left_im, right_im),
        product(left_re, right_im) + product(left_im, right_re),
    )


def phase_table(first, second, modulus):
    angle = (
        2.0 * math.pi / modulus * (first[:, None] * second[None, :] % modulus).astype(jnp.float32)
    )
    return (jnp.cos(angle), jnp.sin(angle))


def along_rows(field):
    lines = field.shape[1]
    plen = GRID // QLEN
    outer_idx = jnp.arange(QLEN, dtype=jnp.int32)
    inner_idx = jnp.arange(plen, dtype=jnp.int32)
    outer_re, outer_im = phase_table(outer_idx, outer_idx, QLEN)
    turn_re, turn_im = phase_table(outer_idx, inner_idx, GRID)
    inner_re, inner_im = phase_table(inner_idx, inner_idx, plen)
    field_re = field[0].reshape(lines, QLEN, plen)
    field_im = field[1].reshape(lines, QLEN, plen)
    middle_re, middle_im = complex_product("kq,rqp->rkp", outer_re, outer_im, field_re, field_im)
    middle_re, middle_im = (
        middle_re * turn_re - middle_im * turn_im,
        middle_re * turn_im + middle_im * turn_re,
    )
    result_re, result_im = complex_product("rkp,pb->rbk", middle_re, middle_im, inner_re, inner_im)
    return jnp.stack([result_re.reshape(lines, GRID), result_im.reshape(lines, GRID)])


def along_columns(field, source_order):
    width = field.shape[2]
    plen = GRID // QLEN
    outer_idx = jnp.arange(QLEN, dtype=jnp.int32)
    inner_idx = jnp.arange(plen, dtype=jnp.int32)
    outer_re, outer_im = phase_table(outer_idx, source_order, QLEN)
    turn_re, turn_im = phase_table(outer_idx, inner_idx, GRID)
    inner_re, inner_im = phase_table(inner_idx, inner_idx, plen)
    field_re = field[0].reshape(QLEN, plen, width)
    field_im = field[1].reshape(QLEN, plen, width)
    middle_re, middle_im = complex_product("bk,kpa->bpa", outer_re, outer_im, field_re, field_im)
    turn_re = turn_re[:, :, None]
    turn_im = turn_im[:, :, None]
    middle_re, middle_im = (
        middle_re * turn_re - middle_im * turn_im,
        middle_re * turn_im + middle_im * turn_re,
    )
    result_re, result_im = complex_product("kpa,pb->abk", middle_re, middle_im, inner_re, inner_im)
    scale = 1.0 / GRID
    return jnp.stack(
        [result_re.reshape(width, GRID) * scale, result_im.reshape(width, GRID) * scale]
    )


def local(visibilities, owner, tile_slot, kernel_index, kernels):
    groups = lax.axis_size("grp")
    owners = lax.axis_size("dev")
    devices = groups * owners
    rows_here = visibilities.shape[0]
    capacity = 2 * rows_here // devices
    target = owner[:, 0]
    onehot = (target[:, None] == jnp.arange(devices, dtype=jnp.int32)[None, :]).astype(jnp.int32)
    slot_rank = jnp.sum((jnp.cumsum(onehot, axis=0) - 1) * onehot, axis=1)
    position = target * capacity + slot_rank
    total_rows = devices * capacity
    vis_out = jnp.zeros((total_rows, 2, VIS), jnp.bfloat16).at[position].set(visibilities)
    labels = jnp.concatenate([tile_slot[:, None], kernel_index], axis=1)
    label_out = jnp.zeros((total_rows, 3), jnp.int32).at[position].set(labels)
    vis_in, label_in = (
        lax.all_to_all(
            vis_out.reshape(devices, capacity, 2, VIS),
            ("grp", "dev"),
            split_axis=0,
            concat_axis=0,
            tiled=True,
        ),
        lax.all_to_all(
            label_out.reshape(devices, capacity, 3),
            ("grp", "dev"),
            split_axis=0,
            concat_axis=0,
            tiled=True,
        ),
    )
    vis_in = vis_in.reshape(total_rows, 2, VIS)
    label_in = label_in.reshape(total_rows, 3)
    slab = GRID // devices
    tile_rows = slab // TILE
    tile_cols = GRID // TILE
    block_rows = min(256, total_rows)
    block_count = total_rows // block_rows

    def grid_block(block_index, uv_tiles):
        first_row = block_index * block_rows
        vis_block = lax.dynamic_slice_in_dim(vis_in, first_row, block_rows, 0)
        label_block = lax.dynamic_slice_in_dim(label_in, first_row, block_rows, 0)
        left_kernel = jnp.take(kernels[0], label_block[:, 1], axis=0)
        right_kernel = jnp.take(kernels[1], label_block[:, 2], axis=0)
        weighted = (
            left_kernel.astype(jnp.float32)[:, None, :, :]
            * vis_block.astype(jnp.float32)[:, :, None, :]
        ).astype(jnp.bfloat16)
        terms = jnp.einsum(
            "rcik,rjk->rcij", weighted, right_kernel, preferred_element_type=jnp.float32
        )
        return uv_tiles.at[label_block[:, 0]].add(terms)

    empty = jnp.zeros((tile_rows * tile_cols, 2, TILE, TILE), jnp.float32)
    uv_tiles = lax.fori_loop(0, block_count, grid_block, empty)
    grid_rows = uv_tiles.reshape(tile_rows, tile_cols, 2, TILE, TILE).transpose(2, 0, 3, 1, 4)
    grid_rows = grid_rows.reshape(2, slab, GRID)
    half = along_rows(grid_rows)
    columns = lax.all_to_all(half, ("grp", "dev"), split_axis=2, concat_axis=1, tiled=True)
    source_order = jnp.arange(QLEN, dtype=jnp.int32)
    return along_columns(columns, source_order)


def solution(mesh):
    return jax.shard_map(
        local,
        mesh=mesh,
        in_specs=(
            P(("grp", "dev"), None, None),
            P(("grp", "dev"), None),
            P(("grp", "dev")),
            P(("grp", "dev"), None),
            P(),
        ),
        out_specs=P(None, ("grp", "dev"), None),
        check_vma=False,
    )
```

profile of v0, /device:TPU:0, one launch (start us, length us, event | category | flops | bytes accessed | tf_op | source)
XLA Modules:
  0.0 1190.8 jit_solution(2324823761991537444)
XLA Ops:
  15.5 49.6 %scatter_fusion.1 = bf16[1024,2,128]{2,1,0:T(2,128)(2,1)} fusion(bf16[1024,2,128]{2,1,0:T(2,128)(2,1)} %broadcast_in_dim.29, s32[512]{0:T(512)S(1)} %bitcast.149, bf16[512,2,128]{2,1,0:T(2,128)(2,1)} %param.9), kind=kCustom, calls=%fused_computation.4 | custom fusion | bytes 788480 | tf_op jit(solution)/shard_map/scatter | solution.py:86
  72.1 15.5 %all-to-all-done.1 = bf16[32,32,2,128]{3,2,1,0:T(2,128)(2,1)S(1)} async-done(((bf16[32,32,2,128]{3,2,1,0:T(2,128)(2,1)}), bf16[32,32,2,128]{3,2,1,0:T(2,128)(2,1)S(1)}, u32[]{:S(2)}, u32[]{:S(2)}) %all-to-all-start.1) | async-done | bytes 524320 | tf_op jit(solution)/shard_map/all_to_all | solution.py:90
  98.8 296.0 %while.13 = (s32[]{:T(128)}, f32[512,2,64,64]{3,2,1,0:T(8,128)}, s32[1024,3]{0,1:T(4,128)S(1)}, bf16[2,32,64,128]{3,2,1,0:T(8,128)(2,1)S(1)}, bf16[1024,2,128]{2...) while((s32[]{:T(128)}, f32[512,2,64,64]{3,2,1,0:T(8,128)}, ...), condition=%wide.region_7.9_spmd, body=%wide.region_5.0_spmd.sunk | while | flops 553721088 | bytes 78276800 | solution.py:129
  120.9 51.7 %scatter_fusion = f32[512,2,64,64]{3,2,1,0:T(8,128)} fusion(f32[512,2,64,64]{3,2,1,0:T(8,128)} %get-tuple-element.179, s32[256]{0:T(256)S(1)} %bitcast.141, f32[256,2,64,64]{3,2,1,0:T(8,128)} %fusion.183), kind=kCustom, calls=%fused_computation.2.clone.1 | custom fusion | flops 2097152 | bytes 25166848 | tf_op jit(solution)/shard_map/while/body/eval_jaxpr/scatter-add | solution.py:126
  194.6 51.9 %scatter_fusion = f32[512,2,64,64]{3,2,1,0:T(8,128)} fusion(f32[512,2,64,64]{3,2,1,0:T(8,128)} %get-tuple-element.179, s32[256]{0:T(256)S(1)} %bitcast.141, f32[256,2,64,64]{3,2,1,0:T(8,128)} %fusion.183), kind=kCustom, calls=%fused_computation.2.clone.1 | custom fusion | flops 2097152 | bytes 25166848 | tf_op jit(solution)/shard_map/while/body/eval_jaxpr/scatter-add | solution.py:126
  268.6 52.0 %scatter_fusion = f32[512,2,64,64]{3,2,1,0:T(8,128)} fusion(f32[512,2,64,64]{3,2,1,0:T(8,128)} %get-tuple-element.179, s32[256]{0:T(256)S(1)} %bitcast.141, f32[256,2,64,64]{3,2,1,0:T(8,128)} %fusion.183), kind=kCustom, calls=%fused_computation.2.clone.1 | custom fusion | flops 2097152 | bytes 25166848 | tf_op jit(solution)/shard_map/while/body/eval_jaxpr/scatter-add | solution.py:126
  342.7 52.1 %scatter_fusion = f32[512,2,64,64]{3,2,1,0:T(8,128)} fusion(f32[512,2,64,64]{3,2,1,0:T(8,128)} %get-tuple-element.179, s32[256]{0:T(256)S(1)} %bitcast.141, f32[256,2,64,64]{3,2,1,0:T(8,128)} %fusion.183), kind=kCustom, calls=%fused_computation.2.clone.1 | custom fusion | flops 2097152 | bytes 25166848 | tf_op jit(solution)/shard_map/while/body/eval_jaxpr/scatter-add | solution.py:126
  394.8 29.5 %copy.85 = f32[4,128,2,64,64]{1,3,0,4,2:T(8,128)} copy(f32[4,128,2,64,64]{4,3,2,1,0:T(8,128)} %bitcast.124) | data formatting | bytes 33554432 | tf_op jit(solution)/shard_map/reshape | solution.py:130
  459.2 18.7 %fusion.8 = (f32[256,128,64]{1,0,2:T(8,128)}, f32[256,128,64]{1,0,2:T(8,128)}) fusion(f32[128,64]{0,1:T(8,128)S(1)} %copy-done.6, f32[128,64]{0,1:T(8,128)S(1)} %copy-done.7, f32[256,64,128]{2,0,1:T(8,128)} %fusion.51, f32[256,64,128]{2,0,1:T(8,128)} %fusion.59, f32[256,64,128]{2,0,1:T(8,128)} %fusion.53, f32[256,128,64]{1,0,2:T(8,128)} %bitcast.128), kind=kOutput, calls=%fused_computation.29 | convolution fusion | flops 3238232064 | bytes 50397184 | tf_op jit(solution)/shard_map/kq,rqp->rkp/dot_general | solution.py:17
  477.9 15.6 %fusion.28 = f32[64,256,128]{2,0,1:T(8,128)S(1)} fusion(f32[256,128,64]{1,0,2:T(8,128)} %get-tuple-element.119), kind=kOutput, calls=%fused_computation.57 | convolution fusion | flops 1610670080 | bytes 16777216 | tf_op jit(solution)/shard_map/rkp,pb->rbk/dot_general | solution.py:17
  493.5 17.2 %fusion.26 = f32[64,256,128]{2,0,1:T(8,128)} fusion(f32[256,128,64]{1,0,2:T(8,128)S(1)} %copy-done.2), kind=kOutput, calls=%fused_computation.55 | convolution fusion | flops 1610670080 | bytes 16777216 | tf_op jit(solution)/shard_map/rkp,pb->rbk/dot_general | solution.py:17
  510.7 17.2 %subtract_bitcast_fusion = f32[256,64,128]{2,1,0:T(8,128)} fusion(f32[64,256,128]{2,0,1:T(8,128)S(1)} %fusion.28, f32[256,128,64]{1,0,2:T(8,128)S(1)} %bitcast.130), kind=kOutput, calls=%fused_computation.38 | convolution fusion | flops 1612767232 | bytes 25165824 | tf_op jit(solution)/shard_map/rkp,pb->rbk/dot_general | solution.py:17
  537.3 18.0 %copy.90 = f32[1,256,8192]{1,0,2:T(1,128)} copy(f32[1,256,8192]{2,1,0:T(8,128)} %stack_reshape.6) | data formatting | bytes 16777216 | tf_op jit(solution)/shard_map/stack;reshape | solution.py:48
  555.3 19.0 %add_bitcast_fusion = f32[256,64,128]{2,1,0:T(8,128)} fusion(f32[64,256,128]{2,0,1:T(8,128)} %fusion.26, f32[256,128,64]{1,0,2:T(8,128)} %get-tuple-element.118), kind=kOutput, calls=%fused_computation.37 | convolution fusion | flops 1612767232 | bytes 25165824 | tf_op jit(solution)/shard_map/rkp,pb->rbk/dot_general | solution.py:17
  583.7 18.1 %copy.91 = f32[1,256,8192]{1,0,2:T(1,128)} copy(f32[1,256,8192]{2,1,0:T(8,128)} %stack_reshape.7) | data formatting | bytes 16777216 | tf_op jit(solution)/shard_map/stack;reshape | solution.py:48
  601.7 16.7 %pad_maximum_fusion = f32[2,256,8192]{1,0,2:T(2,128)S(1)} fusion(f32[1,256,8192]{1,0,2:T(1,128)} %copy.91, f32[1,256,8192]{1,0,2:T(1,128)} %copy.90), kind=kLoop, calls=%fused_computation.25 | loop fusion | flops 4194304 | bytes 33554432 | tf_op jit(solution)/shard_map/stack | solution.py:48
  618.4 373.3 %all_to_all.25 = f32[2,256,8192]{1,0,2:T(2,128)S(1)} all-to-all(f32[2,256,8192]{1,0,2:T(2,128)S(1)} %pad_maximum_fusion), channel_id=1, replica_groups=mesh['grp'=4,'dev'=8] {'grp','dev'}, dimensions={2} | all-to-all | bytes 33554432 | tf_op jit(solution)/shard_map/all_to_all | solution.py:133
  1012.9 17.5 %fusion.22 = f32[128,64,256]{2,0,1:T(8,128)} fusion(f32[128,64,256]{2,1,0:T(8,128)} %bitcast.131), kind=kOutput, calls=%fused_computation.51 | convolution fusion | flops 3221454848 | bytes 16777216 | tf_op jit(solution)/shard_map/bk,kpa->bpa/dot_general | solution.py:17
  1052.6 17.6 %fusion.20 = f32[128,64,256]{2,0,1:T(8,128)} fusion(f32[128,64,256]{2,1,0:T(8,128)} %bitcast.133), kind=kOutput, calls=%fused_computation.49 | convolution fusion | flops 3221454848 | bytes 16777216 | tf_op jit(solution)/shard_map/bk,kpa->bpa/dot_general | solution.py:17
  1070.2 20.2 %multiply_subtract_fusion = (f32[128,64,256]{2,0,1:T(8,128)S(1)}, f32[128,64,256]{2,0,1:T(8,128)S(1)}) fusion(f32[128,64]{0,1:T(8,128)S(1)} %copy-done.6, f32[128,64]{0,1:T(8,128)S(1)} %copy-done.7, f32[128,64,256]{2,0,1:T(8,128)} %fusion.22, f32[128,64,256]{2,0,1:T(8,128)} %fusion.24, f32[128,64,256]{2,0,1:T(8,128)} %fusion.20, f32[128,64,256]{2,1,0:T(8,128)} %bitcast.134), kind=kOutput, calls=%fused_computation.36 | convolution fusion | flops 3238232064 | bytes 50397184 | tf_op jit(solution)/shard_map/bk,kpa->bpa/dot_general | solution.py:17
  1090.4 13.6 %fusion.12 = f32[64,128,256]{2,0,1:T(8,128)} fusion(f32[128,64,256]{2,0,1:T(8,128)S(1)} %get-tuple-element.117), kind=kOutput, calls=%fused_computation.41 | convolution fusion | flops 1610670080 | bytes 16777216 | tf_op jit(solution)/shard_map/kpa,pb->abk/dot_general | solution.py:17
  1117.2 15.9 %multiply_bitcast_fusion.1 = f32[256,64,128]{0,1,2:T(8,128)} fusion(f32[64,128,256]{2,0,1:T(8,128)} %fusion.12, f32[128,64,256]{2,0,1:T(8,128)S(1)} %get-tuple-element.116), kind=kOutput, calls=%fused_computation.34 | convolution fusion | flops 1614864384 | bytes 25165824 | tf_op jit(solution)/shard_map/kpa,pb->abk/dot_general | solution.py:17
  1144.7 14.1 %multiply_bitcast_fusion = f32[256,64,128]{0,1,2:T(8,128)} fusion(f32[64,128,256]{2,0,1:T(8,128)S(1)} %copy-done.3, f32[128,64,256]{2,0,1:T(8,128)S(1)} %get-tuple-element.116), kind=kOutput, calls=%fused_computation.33 | convolution fusion | flops 1614864384 | bytes 25165824 | tf_op jit(solution)/shard_map/kpa,pb->abk/dot_general | solution.py:17
  1173.1 17.5 %copy.105 = f32[2,256,8192]{2,1,0:T(8,128)} copy(f32[2,256,8192]{1,2,0:T(8,128)} %pad_maximum_fusion.1) | data formatting | bytes 33554432 | tf_op jit(solution)/shard_map/stack | solution.py:70
  (107 shorter events, 258.1 us)
Async XLA Ops:
  7.2 58.0 %all-to-all-start = ((s32[32,32,3]{1,2,0:T(4,128)}), s32[32,32,3]{1,2,0:T(4,128)S(1)}, u32[]{:S(2)}, u32[]{:S(2)}) async-start(s32[32,32,3]{1,2,0:T(4,128)} %copy.83), calls=%async_computation | async-start | bytes 131072 | tf_op jit(solution)/shard_map/all_to_all | solution.py:97
  65.2 22.3 %all-to-all-start.1 = ((bf16[32,32,2,128]{3,2,1,0:T(2,128)(2,1)}), bf16[32,32,2,128]{3,2,1,0:T(2,128)(2,1)S(1)}, u32[]{:S(2)}, u32[]{:S(2)}) async-start(bf16[32,32,2,128]{3,2,1,0:T(2,128)(2,1)} %bitcast.16), calls=%async_computation.1 | async-start | bytes 1048576 | tf_op jit(solution)/shard_map/all_to_all | solution.py:90
  87.5 11.3 copy-start.5
  431.0 18.9 %copy-start = (f32[1,4,64,128,64]{3,2,1,4,0:T(8,128)}, f32[1,4,64,128,64]{3,2,1,4,0:T(8,128)S(1)}, u32[]{:S(2)}) copy-start(f32[1,4,64,128,64]{3,2,1,4,0:T(8,128)S(1)} %get-tuple-element.123) | copy-start | bytes 25165828
  449.9 9.3 copy-start.6
  449.9 9.3 copy-start.7
  477.9 15.7 %copy-start.2 = (f32[256,128,64]{1,0,2:T(8,128)S(1)}, f32[256,128,64]{1,0,2:T(8,128)}, u32[]{:S(2)}) copy-start(f32[256,128,64]{1,0,2:T(8,128)} %get-tuple-element.119) | copy-start | bytes 25165828
  477.9 32.8 %slice-start = ((s8[8388608]{0:T(1024)(128)(4,1)}), s8[4194304]{0:T(1024)(128)(4,1)S(1)}, s32[]{:S(2)}) async-start(s8[8388608]{0:T(1024)(128)(4,1)} %bitcast.129), calls=%async_computation.3 | async-start | bytes 8388608
  493.5 17.2 %slice-start.1 = ((s8[8388608]{0:T(1024)(128)(4,1)}), s8[4194304]{0:T(1024)(128)(4,1)S(1)}, s32[]{:S(2)}) async-start(s8[8388608]{0:T(1024)(128)(4,1)} %bitcast.129), calls=%async_computation.4 | async-start | bytes 8388608
  1012.9 17.5 %copy-start.1 = (f32[1,32,256,256]{3,2,1,0:T(8,128)S(1)}, f32[1,32,256,256]{3,2,1,0:T(8,128)}, u32[]{:S(2)}) copy-start(f32[1,32,256,256]{3,2,1,0:T(8,128)} %copy.93) | copy-start | bytes 25165828
  1133.0 11.6 copy-start.3
  1158.7 8.4 copy-start.4
where the time goes:
time: 1200 us; the launch traced here: 1190 us
  blocking collectives  373 us (31%)
  matrix products  283 us (24%)
  other arithmetic  257 us (21%)
  local copies, waits for them, and re-layouts  248 us (21%)
  waiting for transfers between devices  15.5 us (1%)
  starting transfers between devices  13.3 us (1%)
    all_to_all x1, blocking collectives, local(): lax.all_to_all(half, ('grp', 'dev'), split_axis=2, concat_axis=1, tiled=T...  373 us
    dot_general x16, matrix products, product(): return jnp.einsum(pattern, first, second, precision=lax.Precision.HIGHEST)  241 us
    scatter-add x4, other arithmetic, grid_block(): return uv_tiles.at[label_block[:, 0]].add(terms)  208 us
    another operation x4, local copies, waits for them, and re-layouts, along_rows(): jnp.stack([result_re.reshape(lines, GRID), result_im.reshape(lines, GRID)])  54.8 us
    scatter x1, local copies, waits for them, and re-layouts, local(): jnp.zeros((total_rows, 2, VIS), jnp.bfloat16).at[position].set(visibilities)  49.6 us
    dot_general x4, matrix products, grid_block(): jnp.einsum('rcik,rjk->rcij', weighted, right_kernel, preferred_element_ty...  41.5 us
    reshape x1, local copies, waits for them, and re-layouts, local(): uv_tiles.reshape(tile_rows, tile_cols, 2, TILE, TILE)  29.5 us
  transfers between devices with their start and end apart: 2, of which 1 were waited for; matrix products, arithmetic and copies ran while one was open for 4% of the time, Pallas kernels for 0%

commit v1 on v0

v1 whole, which is shorter than its diff:
```python
import jax
import jax.numpy as jnp
import ml_dtypes
import numpy as np
from jax import lax
from jax.experimental import pallas as pl
from jax.experimental.pallas import tpu as pltpu
from jax.sharding import PartitionSpec as P

GRID = 8192
TILE = 64
VIS = 128
COARSE = GRID // TILE
GROUP = 8
STEP = 16
AXES = ("grp", "dev")


def wave(first, second, modulus):
    angle = 2.0 * np.pi / modulus * (np.outer(first, second) % modulus)
    return np.cos(angle), np.sin(angle)


def halves(table):
    high = table.astype(ml_dtypes.bfloat16)
    low = (table - high.astype(np.float64)).astype(ml_dtypes.bfloat16)
    return high, low


def tables(per_device):
    coarse, fine = np.arange(COARSE), np.arange(TILE)
    long_re, long_im = wave(coarse, coarse, COARSE)
    turn_re, turn_im = wave(coarse, fine, GRID)
    short_re, short_im = wave(fine, fine, TILE)
    row_first = halves(np.concatenate([long_re, long_im], axis=1))
    row_turn = (
        np.concatenate([turn_re, turn_re], axis=1).astype(np.float32),
        np.concatenate([-turn_im, turn_im], axis=1).astype(np.float32),
    )
    as_real = np.stack(
        [np.concatenate([short_re, -short_im], axis=1), np.concatenate([short_im, short_re], axis=1)]
    )
    as_real = as_real.reshape(2, TILE // per_device, per_device, 2 * TILE)
    high, low = halves(as_real.transpose(1, 0, 2, 3).reshape(2 * TILE, 2 * TILE))
    row_second = (np.concatenate([high, high], axis=1), low)
    col_first = halves(
        np.concatenate(
            [
                np.concatenate([long_re, long_im], axis=1),
                np.concatenate([-long_im, long_re], axis=1),
            ],
            axis=0,
        )
    )
    col_turn = (turn_re.T.astype(np.float32), turn_im.T.astype(np.float32))
    stacked = np.concatenate(
        [np.concatenate([short_re, -short_im], axis=1), np.concatenate([short_im, short_re], axis=1)],
        axis=0,
    )
    high, low = halves(stacked / GRID)
    col_second = (np.concatenate([high, high], axis=1), low)
    return row_first, row_turn, row_second, col_first, col_turn, col_second


def mm(left, right, dims=((1,), (0,))):
    return lax.dot_general(left, right, (dims, ((), ())), preferred_element_type=jnp.float32)


def split(values):
    high = values.astype(jnp.bfloat16)
    return high, (values - high.astype(jnp.float32)).astype(jnp.bfloat16)


def row_kernel(
    tile_ref, left_ref, right_ref, valid_ref, vis_ref, ka_ref, kb_ref, eh_ref, el_ref,
    wre_ref, wim_ref, fh_ref, fl_ref, out_ref, grid_ref, turn_ref,
):
    tiles = grid_ref.shape[0] // TILE
    rows = vis_ref.shape[0]

    @pl.loop(0, tiles)
    def _(tile):
        grid_ref[pl.ds(pl.multiple_of(tile * TILE, TILE), TILE), :] = jnp.zeros(
            (TILE, 2 * TILE), jnp.float32
        )

    @pl.loop(0, rows // GROUP)
    def _(group):
        first = group * GROUP

        @pl.when(valid_ref[first] > 0)
        def _():
            vis = vis_ref[pl.ds(pl.multiple_of(first, GROUP), GROUP), :]
            terms = []
            for n in range(GROUP):
                left = ka_ref[left_ref[first + n]].astype(jnp.float32)
                weighted = (left * vis[n : n + 1, :]).astype(jnp.bfloat16)
                terms.append(mm(weighted, kb_ref[right_ref[first + n]]))
            for n in range(GROUP):
                at = pl.ds(pl.multiple_of(tile_ref[first + n] * TILE, TILE), TILE)
                grid_ref[at, :] = grid_ref[at, :] + terms[n]

    lane = lax.broadcasted_iota(jnp.int32, (1, 2 * TILE), 1)
    sign = jnp.where(lane < TILE, -1.0, 1.0).astype(jnp.float32)
    span = COARSE * TILE
    pairs = 2

    @pl.loop(0, out_ref.shape[1] // STEP)
    def _(block):
        line0 = block * STEP

        @pl.loop(0, STEP // (2 * pairs))
        def _(part):
            for pair in range(pairs):
                columns = []
                for n in range(2):
                    line = line0 + part * (2 * pairs) + pair * 2 + n
                    start = (line // TILE) * span + line % TILE
                    cells = grid_ref[pl.ds(start, COARSE, stride=TILE), :]
                    swapped = pltpu.roll(cells, TILE, axis=1) * sign
                    columns.append(jnp.concatenate([cells, swapped], axis=0).astype(jnp.bfloat16))
                both = jnp.concatenate(columns, axis=1)
                middle = mm(eh_ref[...], both) + mm(el_ref[...], both)
                for n in range(2):
                    value = middle[:, n * 2 * TILE : (n + 1) * 2 * TILE]
                    value = value * wre_ref[...] + pltpu.roll(value, TILE, axis=1) * wim_ref[...]
                    high, low = split(value)
                    result = mm(
                        fh_ref[...], jnp.concatenate([high, low], axis=1), ((1,), (1,))
                    ) + mm(fl_ref[...], high, ((1,), (1,)))
                    turn_ref[
                        pl.ds(part * (2 * pairs) + pair * 2 + n, 2 * TILE, stride=STEP), :
                    ] = result

        out_ref[:, pl.ds(pl.multiple_of(line0, STEP), STEP), :] = (
            turn_ref[...].reshape(2 * TILE, STEP, COARSE).astype(jnp.bfloat16)
        )


def column_kernel(
    x_ref, eh_ref, el_ref, wre_ref, wim_ref, fh_ref, fl_ref, out_ref, wide_ref, mid_ref, turn_ref
):
    sources, lines = x_ref.shape[0], x_ref.shape[3]

    @pl.loop(0, sources)
    def _(source):
        at = pl.ds(pl.multiple_of(source * lines, lines), lines)
        for c in range(2):
            wide_ref[c, at, :] = x_ref[source, c, 0].astype(jnp.float32)

    @pl.loop(0, TILE // 2)
    def _(half):
        for n in range(2):
            i = half * 2 + n
            cells = jnp.concatenate(
                [wide_ref[c, pl.ds(i, COARSE, stride=TILE), :] for c in range(2)], axis=0
            ).astype(jnp.bfloat16)
            middle = mm(cells, eh_ref[...], ((0,), (0,))) + mm(cells, el_ref[...], ((0,), (0,)))
            re, im = middle[:, :COARSE], middle[:, COARSE:]
            wre, wim = wre_ref[pl.ds(i, 1), :], wim_ref[pl.ds(i, 1), :]
            mid_ref[0, pl.ds(i, COARSE, stride=TILE), :] = re * wre - im * wim
            mid_ref[1, pl.ds(i, COARSE, stride=TILE), :] = re * wim + im * wre

    @pl.loop(0, COARSE // 8)
    def _(block):
        for n in range(8):
            at = pl.ds(pl.multiple_of((block * 8 + n) * TILE, TILE), TILE)
            cells = jnp.concatenate([mid_ref[c, at, :] for c in range(2)], axis=0)
            high, low = split(cells)
            result = mm(fh_ref[...], jnp.concatenate([high, low], axis=0)) + mm(fl_ref[...], high)
            turn_ref[pl.ds(n, 2 * TILE, stride=8), :] = result
        rows = pl.ds(pl.multiple_of(block * 8, 8), 8)
        for c in range(2):
            for m in range(TILE):
                out_ref[c, rows, m * COARSE : (m + 1) * COARSE] = turn_ref[
                    (c * TILE + m) * 8 : (c * TILE + m + 1) * 8, :
                ]


def local(visibilities, owner, tile_slot, kernel_index, kernels):
    devices = lax.axis_size("grp") * lax.axis_size("dev")
    rows_here = visibilities.shape[0]
    capacity = 2 * rows_here // devices
    total = devices * capacity
    lines = GRID // devices
    width = GRID // devices
    blocks = max(1, width // COARSE)
    row_first, row_turn, row_second, col_first, col_turn, col_second = tables(blocks)

    target = owner[:, 0]
    onehot = target[:, None] == jnp.arange(devices, dtype=jnp.int32)[None, :]
    index = jnp.arange(rows_here, dtype=jnp.int32)
    before = (index[:, None] > index[None, :]).astype(jnp.bfloat16)
    ranks = mm(before, onehot.astype(jnp.bfloat16))
    rank = jnp.sum(jnp.where(onehot, ranks, 0.0), axis=1).astype(jnp.int32)
    position = target * capacity + rank
    place = (jnp.arange(total, dtype=jnp.int32)[:, None] == position[None, :]).astype(jnp.bfloat16)
    labels = jnp.stack(
        [
            tile_slot // COARSE,
            tile_slot % COARSE,
            kernel_index[:, 0],
            kernel_index[:, 1],
            jnp.ones_like(tile_slot),
        ],
        axis=1,
    ).astype(jnp.bfloat16)
    payload = jnp.concatenate(
        [
            visibilities.reshape(rows_here, 2 * VIS),
            jnp.pad(labels, ((0, 0), (0, VIS - labels.shape[1]))),
        ],
        axis=1,
    )
    sent = mm(place, payload).astype(jnp.bfloat16).reshape(devices, capacity, 3 * VIS)
    got = lax.all_to_all(sent, AXES, split_axis=0, concat_axis=0, tiled=True)
    got = got.reshape(total, 3 * VIS)
    vis_in = got[:, : 2 * VIS].astype(jnp.float32)
    label_in = got[:, 2 * VIS : 2 * VIS + 5].astype(jnp.int32)
    tile_in = label_in[:, 0] * COARSE + label_in[:, 1]

    left = jnp.concatenate([kernels[0], kernels[0]], axis=2)
    right = jnp.swapaxes(kernels[1], 1, 2)
    empty = jnp.zeros_like(right)
    right = jnp.concatenate(
        [jnp.concatenate([right, empty], axis=2), jnp.concatenate([empty, right], axis=2)], axis=1
    )
    smem = pl.BlockSpec(memory_space=pltpu.SMEM)
    vmem = pl.BlockSpec(memory_space=pltpu.VMEM)
    half = pl.pallas_call(
        row_kernel,
        out_shape=jax.ShapeDtypeStruct((2 * TILE, lines, COARSE), jnp.bfloat16),
        in_specs=[smem] * 4 + [vmem] * 9,
        out_specs=vmem,
        scratch_shapes=[
            pltpu.VMEM((lines * COARSE, 2 * TILE), jnp.float32),
            pltpu.VMEM((2 * TILE * STEP, COARSE), jnp.float32),
        ],
        compiler_params=pltpu.CompilerParams(vmem_limit_bytes=52 << 20),
        name="grid_rows",
    )(
        tile_in, label_in[:, 2], label_in[:, 3], label_in[:, 4], vis_in, left, right,
        *row_first, *row_turn, *row_second,
    )
    narrow = min(width, COARSE)
    if narrow < COARSE:
        parts = COARSE // narrow
        half = half.reshape(TILE, 2, lines, parts, narrow).transpose(0, 3, 1, 2, 4)
    half = half.reshape(devices, 2, blocks, lines, narrow)
    columns = lax.all_to_all(half, AXES, split_axis=0, concat_axis=0, tiled=True)
    if narrow < COARSE:
        columns = jnp.pad(columns, ((0, 0),) * 4 + ((0, COARSE - narrow),))
    fixed = lambda table: pl.BlockSpec(table.shape, lambda b: (0,) * table.ndim)
    constants = (*col_first, *col_turn, *col_second)
    image = pl.pallas_call(
        column_kernel,
        grid=(blocks,),
        out_shape=jax.ShapeDtypeStruct((2, blocks * COARSE, GRID), jnp.float32),
        in_specs=[pl.BlockSpec((devices, 2, 1, lines, COARSE), lambda b: (0, 0, b, 0, 0))]
        + [fixed(table) for table in constants],
        out_specs=pl.BlockSpec((2, COARSE, GRID), lambda b: (0, b, 0)),
        scratch_shapes=[
            pltpu.VMEM((2, GRID, COARSE), jnp.float32),
            pltpu.VMEM((2, TILE * COARSE, COARSE), jnp.float32),
            pltpu.VMEM((2 * TILE * 8, COARSE), jnp.float32),
        ],
        compiler_params=pltpu.CompilerParams(
            dimension_semantics=("arbitrary",), vmem_limit_bytes=56 << 20
        ),
        name="columns",
    )(columns, *constants)
    return image[:, :width]


def solution(mesh):
    return jax.shard_map(
        local,
        mesh=mesh,
        in_specs=(
            P(AXES, None, None),
            P(AXES, None),
            P(AXES),
            P(AXES, None),
            P(),
        ),
        out_specs=P(None, AXES, None),
        check_vma=False,
    )
```

time: 1200 us -> 391 us (0.33)
  matrix products: 283 us -> 2.62 us
  other arithmetic: 257 us -> 6.48 us
  local copies, waits for them, and re-layouts: 248 us -> 1.86 us
  blocking collectives: 373 us -> 189 us
  Pallas kernels: 0 us -> 166 us
    dot_general x20 -> x2, matrix products: 283 us -> 2.62 us  [mm(): lax.dot_general(left, right, (dims, ((), ())), preferred_element_type=jnp...]
    scatter-add x4 -> x0, other arithmetic: 208 us -> none  [grid_block(): return uv_tiles.at[label_block[:, 0]].add(terms)]
    all_to_all x1, blocking collectives: 373 us -> 189 us  [local(): lax.all_to_all(half, AXES, split_axis=0, concat_axis=0, tiled=True)]
    pallas_call x0 -> x2, Pallas kernels: none -> 166 us  [the longest x1 109 us: local(): pl.pallas_call(row_kernel, out_shape=jax.ShapeDtypeStruct((2 * TILE, line...]
    another operation x7 -> x3, local copies, waits for them, and re-layouts: 72.5 us -> 0.09 us  [local(): jnp.stack([tile_slot // COARSE, tile_slot % COARSE, kernel_index[:, 0], k...]
    scatter x2 -> x0, local copies, waits for them, and re-layouts: 51.5 us -> none  [the longest x1 49.6 us: local(): jnp.zeros((total_rows, 2, VIS), jnp.bfloat16).at[position].set(visibilities)]
    slice x4 -> x1, local copies, waits for them, and re-layouts: 31.1 us -> 0.07 us  [local(): right = jnp.swapaxes(kernels[1], 1, 2)]
    reshape x3 -> x0, local copies, waits for them, and re-layouts: 30.4 us -> none  [the longest x1 29.5 us: local(): uv_tiles.reshape(tile_rows, tile_cols, 2, TILE, TILE)]
  transfers between devices with their start and end apart: 2 -> 1, of which waited for: 1 -> 1; matrix products, arithmetic and copies ran while one was open for 4% -> 1% of each run, Pallas kernels for 0% -> 0%
where the time goes in v1:
time: 391 us; the launch traced here: 392 us
  blocking collectives  189 us (48%)
  Pallas kernels  166 us (42%)
  waiting for transfers between devices  18.4 us (5%)
  starting transfers between devices  7.3 us (2%)
  other arithmetic  6.48 us (2%)
    all_to_all x1, blocking collectives, local(): lax.all_to_all(half, AXES, split_axis=0, concat_axis=0, tiled=True)  189 us
    pallas_call x1, Pallas kernels, local(): pl.pallas_call(row_kernel, out_shape=jax.ShapeDtypeStruct((2 * TILE, line...  109 us
    pallas_call x1, Pallas kernels, local(): pl.pallas_call(column_kernel, grid=(blocks,), out_shape=jax.ShapeDtypeStr...  57.8 us
    all_to_all x1, waiting for transfers between devices, local(): got = lax.all_to_all(sent, AXES, split_axis=0, concat_axis=0, tiled=True)  18.4 us
  transfers between devices with their start and end apart: 1, of which 1 were waited for; matrix products, arithmetic and copies ran while one was open for 1% of the time, Pallas kernels for 0%

profile of v1, /device:TPU:0, one launch (start us, length us, event | category | flops | bytes accessed | tf_op | source)
XLA Modules:
  0.0 391.8 jit_solution(2454707342442807289)
XLA Ops:
  0.0 1.0 fusion.5
  1.0 0.7 convert_add_fusion
  1.7 0.7 convert.15
  2.4 0.7 fusion.16
  3.1 0.1 pad.16.clone
  3.2 0.1 maximum_maximum_fusion
  3.3 0.2 copy.25
  3.5 1.0 copy.28
  4.5 1.6 fusion.4
  6.1 7.3 %all-to-all-start = ((bf16[32,32,384]{2,1,0:T(8,128)(2,1)}), bf16[32,32,384]{2,1,0:T(8,128)(2,1)S(1)}, u32[]{:S(2)}, u32[]{:S(2)}) async-start(bf16[32,32,384]{2,1,0:T(8,128)(2,1)} %bitcast.1), calls=%async_computation | async-start | bytes 1572864 | tf_op jit(solution)/shard_map/all_to_all | solution.py:216
  13.4 0.1 fusion.22
  13.5 0.5 copy.24
  13.9 1.1 pad_maximum_fusion.ka_ref
  15.0 2.0 fusion.2.kb_ref
  17.0 18.4 %all-to-all-done = bf16[32,32,384]{2,1,0:T(8,128)(2,1)S(1)} async-done(((bf16[32,32,384]{2,1,0:T(8,128)(2,1)}), bf16[32,32,384]{2,1,0:T(8,128)(2,1)S(1)}, u32[]{:S(2)}, u32[]{:S(2)}) %all-to-all-start) | async-done | bytes 786464 | tf_op jit(solution)/shard_map/all_to_all | solution.py:216
  35.3 0.1 slice_convert_fusion.1
  35.4 0.0 copy-start
  35.4 0.0 copy-start.1
  35.4 0.0 copy-start.2
  35.5 0.1 slice_convert_fusion.vis_ref
  35.5 1.2 slice_reduce_fusion
  36.8 108.7 %grid_rows.1 = bf16[128,256,128]{2,1,0:T(8,128)(2,1)} custom-call(s32[1024]{0:T(1024)S(1)} %get-tuple-element.8.tile_ref, s32[1024]{0:T(1024)S(1)} %get-tuple-element.7.left_ref, s32[1024]{0:T(1024)S(1)} %get-tuple-element.6.right_ref, s32[1024]{0:T(1024)S(1)} %get-tuple-element.5.valid_ref, f32[1024,256]{1,0:T(8,128)S(1)} %slice_convert_fusion.vis_ref, ...), custom_call_target="tpu_custom_call" | custom-call | tf_op jit(solution)/shard_map/grid_rows/pallas_call | solution.py:230
  145.5 188.5 %all_to_all.10.x_ref = bf16[32,2,2,256,128]{4,3,2,1,0:T(8,128)(2,1)} all-to-all(bf16[32,2,2,256,128]{4,3,2,1,0:T(8,128)(2,1)} %bitcast.14), channel_id=1, replica_groups=mesh['grp'=4,'dev'=8] {'grp','dev'}, dimensions={0} | all-to-all | bytes 16777216 | tf_op jit(solution)/shard_map/all_to_all | solution.py:250
  334.0 57.8 %columns.1 = f32[2,256,8192]{2,1,0:T(8,128)} custom-call(bf16[32,2,2,256,128]{4,3,2,1,0:T(8,128)(2,1)} %all_to_all.10.x_ref, bf16[256,256]{1,0:T(8,128)(2,1)} %constant.70.clone.eh_ref, bf16[256,256]{1,0:T(8,128)(2,1)} %constant.71.clone.el_ref, f32[64,128]{1,0:T(8,128)} %constant.72.clone.wre_ref, f32[64,128]{1,0:T(8,128)} %constant.73.clone.wim_ref, ...), custom_call_target="tpu_custom_call" | custom-call | tf_op jit(solution)/shard_map/columns/pallas_call | solution.py:255
  (13 shorter events, 0.0 us)
Async XLA Ops:
  4.5 8.9 %copy-start.6 = (bf16[2,32,64,128]{3,2,1,0:T(8,128)(2,1)S(1)}, bf16[2,32,64,128]{3,2,1,0:T(8,128)(2,1)}, u32[]{:S(2)}) copy-start(bf16[2,32,64,128]{3,2,1,0:T(8,128)(2,1)} %param.21) | copy-start | bytes 3145732
  6.1 29.3 %all-to-all-start = ((bf16[32,32,384]{2,1,0:T(8,128)(2,1)}), bf16[32,32,384]{2,1,0:T(8,128)(2,1)S(1)}, u32[]{:S(2)}, u32[]{:S(2)}) async-start(bf16[32,32,384]{2,1,0:T(8,128)(2,1)} %bitcast.1), calls=%async_computation | async-start | bytes 1572864 | tf_op jit(solution)/shard_map/all_to_all | solution.py:216
  35.4 1.3 copy-start
  35.4 1.3 copy-start.1
  35.4 1.3 copy-start.2
  35.4 1.3 copy-start.3
  35.4 1.3 copy-start.4
  35.5 1.3 copy-start.5

commit v2 on v1

--- a/solution.py
+++ b/solution.py
@@ -1,3 +1,5 @@
+import functools
+
 import jax
 import jax.numpy as jnp
 import ml_dtypes
@@ -71,9 +73,8 @@
     return high, (values - high.astype(jnp.float32)).astype(jnp.bfloat16)
 
 
-def row_kernel(
-    tile_ref, left_ref, right_ref, valid_ref, vis_ref, ka_ref, kb_ref, eh_ref, el_ref,
-    wre_ref, wim_ref, fh_ref, fl_ref, out_ref, grid_ref, turn_ref,
+def grid_kernel(
+    tile_ref, left_ref, right_ref, valid_ref, vis_ref, ka_ref, kb_ref, grid_ref
 ):
     tiles = grid_ref.shape[0] // TILE
     rows = vis_ref.shape[0]
@@ -100,41 +101,106 @@
                 at = pl.ds(pl.multiple_of(tile_ref[first + n] * TILE, TILE), TILE)
                 grid_ref[at, :] = grid_ref[at, :] + terms[n]
 
+
+def transform_block(grid_ref, tables_of, out_ref, turn_ref, line0):
+    eh_ref, el_ref, wre_ref, wim_ref, fh_ref, fl_ref = tables_of
     lane = lax.broadcasted_iota(jnp.int32, (1, 2 * TILE), 1)
     sign = jnp.where(lane < TILE, -1.0, 1.0).astype(jnp.float32)
     span = COARSE * TILE
     pairs = 2
 
+    @pl.loop(0, STEP // (2 * pairs))
+    def _(part):
+        for pair in range(pairs):
+            columns = []
+            for n in range(2):
+                line = line0 + part * (2 * pairs) + pair * 2 + n
+                start = (line // TILE) * span + line % TILE
+                cells = grid_ref[pl.ds(start, COARSE, stride=TILE), :]
+                swapped = pltpu.roll(cells, TILE, axis=1) * sign
+                columns.append(jnp.concatenate([cells, swapped], axis=0).astype(jnp.bfloat16))
+            both = jnp.concatenate(columns, axis=1)
+            middle = mm(eh_ref[...], both) + mm(el_ref[...], both)
+            for n in range(2):
+                value = middle[:, n * 2 * TILE : (n + 1) * 2 * TILE]
+                value = value * wre_ref[...] + pltpu.roll(value, TILE, axis=1) * wim_ref[...]
+                high, low = split(value)
+                result = mm(
+                    fh_ref[...], jnp.concatenate([high, low], axis=1), ((1,), (1,))
+                ) + mm(fl_ref[...], high, ((1,), (1,)))
+                turn_ref[
+                    pl.ds(part * (2 * pairs) + pair * 2 + n, 2 * TILE, stride=STEP), :
+                ] = result
+
+    out_ref[:, pl.ds(pl.multiple_of(line0, STEP), STEP), :] = (
+        turn_ref[...].reshape(2 * TILE, STEP, COARSE).astype(jnp.bfloat16)
+    )
+
+
+def row_kernel(
+    grid_ref, eh_ref, el_ref, wre_ref, wim_ref, fh_ref, fl_ref, out_ref, turn_ref
+):
+    tables_of = (eh_ref, el_ref, wre_ref, wim_ref, fh_ref, fl_ref)
+
     @pl.loop(0, out_ref.shape[1] // STEP)
     def _(block):
-        line0 = block * STEP
-
-        @pl.loop(0, STEP // (2 * pairs))
-        def _(part):
-            for pair in range(pairs):
-                columns = []
-                for n in range(2):
-                    line = line0 + part * (2 * pairs) + pair * 2 + n
-                    start = (line // TILE) * span + line % TILE
-                    cells = grid_ref[pl.ds(start, COARSE, stride=TILE), :]
-                    swapped = pltpu.roll(cells, TILE, axis=1) * sign
-                    columns.append(jnp.concatenate([cells, swapped], axis=0).astype(jnp.bfloat16))
-                both = jnp.concatenate(columns, axis=1)
-                middle = mm(eh_ref[...], both) + mm(el_ref[...], both)
-                for n in range(2):
-                    value = middle[:, n * 2 * TILE : (n + 1) * 2 * TILE]
-                    value = value * wre_ref[...] + pltpu.roll(value, TILE, axis=1) * wim_ref[...]
-                    high, low = split(value)
-                    result = mm(
-                        fh_ref[...], jnp.concatenate([high, low], axis=1), ((1,), (1,))
-                    ) + mm(fl_ref[...], high, ((1,), (1,)))
-                    turn_ref[
-                        pl.ds(part * (2 * pairs) + pair * 2 + n, 2 * TILE, stride=STEP), :
-                    ] = result
-
-        out_ref[:, pl.ds(pl.multiple_of(line0, STEP), STEP), :] = (
-            turn_ref[...].reshape(2 * TILE, STEP, COARSE).astype(jnp.bfloat16)
+        transform_block(grid_ref, tables_of, out_ref, turn_ref, block * STEP)
+
+
+def send_kernel(
+    groups, owners, grid_ref, eh_ref, el_ref, wre_ref, wim_ref, fh_ref, fl_ref, got_ref,
+    stage_ref, turn_ref, send_sem, recv_sem, own_sem,
+):
+    tables_of = (eh_ref, el_ref, wre_ref, wim_ref, fh_ref, fl_ref)
+    devices = groups * owners
+    strips = stage_ref.shape[1] // TILE
+    share = stage_ref.shape[0] // devices
+    me = lax.axis_index("grp") * owners + lax.axis_index("dev")
+
+    def piece(strip, peer):
+        rows = pl.ds(strip * TILE, TILE)
+        return pltpu.make_async_remote_copy(
+            src_ref=stage_ref.at[pl.ds(peer * share, share), rows, :],
+            dst_ref=got_ref.at[me, :, rows, :],
+            send_sem=send_sem.at[strip, peer],
+            recv_sem=recv_sem.at[strip, me],
+            device_id=(peer // owners, peer % owners),
+            device_id_type=pl.DeviceIdType.MESH,
         )
+
+    def arrival(strip, peer):
+        rows = pl.ds(strip * TILE, TILE)
+        return pltpu.make_async_remote_copy(
+            src_ref=stage_ref.at[pl.ds(peer * share, share), rows, :],
+            dst_ref=got_ref.at[peer, :, rows, :],
+            send_sem=send_sem.at[strip, peer],
+            recv_sem=recv_sem.at[strip, peer],
+            device_id=(peer // owners, peer % owners),
+            device_id_type=pl.DeviceIdType.MESH,
+        )
+
+    own = pltpu.make_async_copy(
+        stage_ref.at[pl.ds(me * share, share), :, :], got_ref.at[me], own_sem
+    )
+    for strip in range(strips):
+        @pl.loop(0, TILE // STEP)
+        def _(block):
+            transform_block(grid_ref, tables_of, stage_ref, turn_ref, strip * TILE + block * STEP)
+
+        @pl.loop(1, devices)
+        def _(n):
+            piece(strip, (me + n) % devices).start()
+
+    own.start()
+    own.wait()
+    for strip in range(strips):
+        @pl.loop(1, devices)
+        def _(n):
+            piece(strip, (me + n) % devices).wait_send()
+
+        @pl.loop(1, devices)
+        def _(n):
+            arrival(strip, (me + n) % devices).wait_recv()
 
 
 def column_kernel(
@@ -227,29 +293,50 @@
     )
     smem = pl.BlockSpec(memory_space=pltpu.SMEM)
     vmem = pl.BlockSpec(memory_space=pltpu.VMEM)
-    half = pl.pallas_call(
-        row_kernel,
-        out_shape=jax.ShapeDtypeStruct((2 * TILE, lines, COARSE), jnp.bfloat16),
-        in_specs=[smem] * 4 + [vmem] * 9,
+    field = pl.pallas_call(
+        grid_kernel,
+        out_shape=jax.ShapeDtypeStruct((lines * COARSE, 2 * TILE), jnp.float32),
+        in_specs=[smem] * 4 + [vmem] * 3,
         out_specs=vmem,
-        scratch_shapes=[
-            pltpu.VMEM((lines * COARSE, 2 * TILE), jnp.float32),
-            pltpu.VMEM((2 * TILE * STEP, COARSE), jnp.float32),
-        ],
-        compiler_params=pltpu.CompilerParams(vmem_limit_bytes=52 << 20),
-        name="grid_rows",
-    )(
-        tile_in, label_in[:, 2], label_in[:, 3], label_in[:, 4], vis_in, left, right,
-        *row_first, *row_turn, *row_second,
-    )
-    narrow = min(width, COARSE)
-    if narrow < COARSE:
-        parts = COARSE // narrow
-        half = half.reshape(TILE, 2, lines, parts, narrow).transpose(0, 3, 1, 2, 4)
-    half = half.reshape(devices, 2, blocks, lines, narrow)
-    columns = lax.all_to_all(half, AXES, split_axis=0, concat_axis=0, tiled=True)
-    if narrow < COARSE:
-        columns = jnp.pad(columns, ((0, 0),) * 4 + ((0, COARSE - narrow),))
+        compiler_params=pltpu.CompilerParams(vmem_limit_bytes=40 << 20),
+        name="grid_cells",
+    )(tile_in, label_in[:, 2], label_in[:, 3], label_in[:, 4], vis_in, left, right)
+    row_tables = (*row_first, *row_turn, *row_second)
+    turned = pltpu.VMEM((2 * TILE * STEP, COARSE), jnp.float32)
+    if width >= COARSE:
+        columns = pl.pallas_call(
+            functools.partial(send_kernel, lax.axis_size("grp"), lax.axis_size("dev")),
+            out_shape=jax.ShapeDtypeStruct((devices, 2 * blocks, lines, COARSE), jnp.bfloat16),
+            in_specs=[vmem] * 7,
+            out_specs=pl.BlockSpec(memory_space=pl.ANY),
+            scratch_shapes=[
+                pltpu.VMEM((2 * TILE, lines, COARSE), jnp.bfloat16),
+                turned,
+                pltpu.SemaphoreType.DMA((lines // TILE, devices)),
+                pltpu.SemaphoreType.DMA((lines // TILE, devices)),
+                pltpu.SemaphoreType.DMA,
+            ],
+            compiler_params=pltpu.CompilerParams(
+                vmem_limit_bytes=52 << 20, has_side_effects=True
+            ),
+            name="rows_sent",
+        )(field, *row_tables)
+        columns = columns.reshape(devices, 2, blocks, lines, COARSE)
+    else:
+        half = pl.pallas_call(
+            row_kernel,
+            out_shape=jax.ShapeDtypeStruct((2 * TILE, lines, COARSE), jnp.bfloat16),
+            in_specs=[vmem] * 7,
+            out_specs=vmem,
+            scratch_shapes=[turned],
+            compiler_params=pltpu.CompilerParams(vmem_limit_bytes=52 << 20),
+            name="rows",
+        )(field, *row_tables)
+        parts = COARSE // width
+        half = half.reshape(TILE, 2, lines, parts, width).transpose(0, 3, 1, 2, 4)
+        half = half.reshape(devices, 2, blocks, lines, width)
+        columns = lax.all_to_all(half, AXES, split_axis=0, concat_axis=0, tiled=True)
+        columns = jnp.pad(columns, ((0, 0),) * 4 + ((0, COARSE - width),))
     fixed = lambda table: pl.BlockSpec(table.shape, lambda b: (0,) * table.ndim)
     constants = (*col_first, *col_turn, *col_second)
     image = pl.pallas_call(

time: 391 us -> 347 us (0.89)
  blocking collectives: 189 us -> 0 us
  Pallas kernels: 166 us -> 307 us
    all_to_all x1 -> x0, blocking collectives: 189 us -> none  [local(): lax.all_to_all(half, AXES, split_axis=0, concat_axis=0, tiled=True)]
    pallas_call x1 -> x2, Pallas kernels: 109 us -> 249 us  [the longest x1 228 us: local(): pl.pallas_call(functools.partial(send_kernel, lax.axis_size('grp'), lax.a...]
where the time goes in v2:
time: 347 us; the launch traced here: 346 us
  Pallas kernels  307 us (88%)
  waiting for transfers between devices  18.7 us (5%)
  starting transfers between devices  7.41 us (2%)
  other arithmetic  6.11 us (2%)
  local copies, waits for them, and re-layouts  3.85 us (1%)
    pallas_call x1, Pallas kernels, local(): pl.pallas_call(functools.partial(send_kernel, lax.axis_size('grp'), lax.a...  228 us
    pallas_call x1, Pallas kernels, local(): pl.pallas_call(column_kernel, grid=(blocks,), out_shape=jax.ShapeDtypeStr...  57.8 us
    pallas_call x1, Pallas kernels, local(): pl.pallas_call(grid_kernel, out_shape=jax.ShapeDtypeStruct((lines * COARS...  20.6 us
    all_to_all x1, waiting for transfers between devices, local(): got = lax.all_to_all(sent, AXES, split_axis=0, concat_axis=0, tiled=True)  18.7 us
    all_to_all x1, starting transfers between devices, local(): got = lax.all_to_all(sent, AXES, split_axis=0, concat_axis=0, tiled=True)  7.41 us
  transfers between devices with their start and end apart: 1, of which 1 were waited for; matrix products, arithmetic and copies ran while one was open for 1% of the time, Pallas kernels for 0%

profile of v2, /device:TPU:0, one launch (start us, length us, event | category | flops | bytes accessed | tf_op | source)
XLA Modules:
  0.0 345.5 jit_solution(3666885495416763764)
XLA Ops:
  0.0 1.0 fusion.5
  1.0 0.7 convert_add_fusion
  1.7 0.7 convert.15
  2.4 0.7 fusion.16
  3.1 0.1 pad.16.clone
  3.2 0.1 maximum_maximum_fusion
  3.3 0.2 copy.25
  3.5 1.0 copy.28
  4.5 1.6 fusion.4
  6.1 7.4 %all-to-all-start = ((bf16[32,32,384]{2,1,0:T(8,128)(2,1)}), bf16[32,32,384]{2,1,0:T(8,128)(2,1)}, u32[]{:S(2)}, u32[]{:S(2)}) async-start(bf16[32,32,384]{2,1,0:T(8,128)(2,1)} %bitcast.1), calls=%async_computation | async-start | bytes 1572864 | tf_op jit(solution)/shard_map/all_to_all | solution.py:282
  13.5 0.1 fusion.22
  13.6 1.3 copy.24
  14.9 0.1 pad_maximum_fusion.ka_ref
  15.0 1.1 copy-done.6
  16.1 0.6 fusion.2.kb_ref
  16.8 18.7 %all-to-all-done = bf16[32,32,384]{2,1,0:T(8,128)(2,1)} async-done(((bf16[32,32,384]{2,1,0:T(8,128)(2,1)}), bf16[32,32,384]{2,1,0:T(8,128)(2,1)}, u32[]{:S(2)}, u32[]{:S(2)}) %all-to-all-start) | async-done | bytes 786464 | tf_op jit(solution)/shard_map/all_to_all | solution.py:282
  35.5 1.0 slice_convert_fusion.1
  36.5 1.1 slice_convert_fusion.vis_ref
  37.6 1.2 slice_reduce_fusion
  38.8 0.0 copy-start.1
  38.8 0.0 copy-start.2
  38.8 20.6 %grid_cells.1.grid_ref = f32[32768,128]{1,0:T(8,128)} custom-call(s32[1024]{0:T(1024)S(1)} %get-tuple-element.8.tile_ref, s32[1024]{0:T(1024)S(1)} %get-tuple-element.7.left_ref, s32[1024]{0:T(1024)S(1)} %get-tuple-element.6.right_ref, s32[1024]{0:T(1024)S(1)} %get-tuple-element.5.valid_ref, f32[1024,256]{1,0:T(8,128)S(1)} %slice_convert_fusion.vis_ref, ...), custom_call_target="tpu_custom_call" | custom-call | tf_op jit(solution)/shard_map/grid_cells/pallas_call | solution.py:296
  59.5 228.2 %rows_sent.1 = bf16[32,4,256,128]{3,2,1,0:T(8,128)(2,1)} custom-call(f32[32768,128]{1,0:T(8,128)} %grid_cells.1.grid_ref, bf16[128,256]{1,0:T(8,128)(2,1)S(1)} %copy-done.4, bf16[128,256]{1,0:T(8,128)(2,1)S(1)} %copy-done.3, f32[128,128]{1,0:T(8,128)S(1)} %copy-done.2, f32[128,128]{1,0:T(8,128)S(1)} %copy-done.1, bf16[128,256]{1,0:T(8,128)(2,1)S(1)} %copy-done, ...), custom_call_target="tpu_custom_call" | custom-call | tf_op jit(solution)/shard_map/rows_sent/pallas_call | solution.py:307
  287.7 57.8 %columns.1 = f32[2,256,8192]{2,1,0:T(8,128)} custom-call(bf16[32,2,2,256,128]{4,3,2,1,0:T(8,128)(2,1)} %bitcast.14, bf16[256,256]{1,0:T(8,128)(2,1)} %constant.70.clone.eh_ref, bf16[256,256]{1,0:T(8,128)(2,1)} %constant.71.clone.el_ref, f32[64,128]{1,0:T(8,128)} %constant.72.clone.wre_ref, f32[64,128]{1,0:T(8,128)} %constant.73.clone.wim_ref, ...), custom_call_target="tpu_custom_call" | custom-call | tf_op jit(solution)/shard_map/columns/pallas_call | solution.py:342
  (15 shorter events, 0.1 us)
Async XLA Ops:
  4.5 9.1 %copy-start.7 = (bf16[2,32,64,128]{3,2,1,0:T(8,128)(2,1)S(1)}, bf16[2,32,64,128]{3,2,1,0:T(8,128)(2,1)}, u32[]{:S(2)}) copy-start(bf16[2,32,64,128]{3,2,1,0:T(8,128)(2,1)} %param.21) | copy-start | bytes 3145732
  6.1 29.4 %all-to-all-start = ((bf16[32,32,384]{2,1,0:T(8,128)(2,1)}), bf16[32,32,384]{2,1,0:T(8,128)(2,1)}, u32[]{:S(2)}, u32[]{:S(2)}) async-start(bf16[32,32,384]{2,1,0:T(8,128)(2,1)} %bitcast.1), calls=%async_computation | async-start | bytes 1572864 | tf_op jit(solution)/shard_map/all_to_all | solution.py:282
  14.9 1.2 copy-start.6
  38.8 20.7 %copy-start = (bf16[128,256]{1,0:T(8,128)(2,1)S(1)}, bf16[128,256]{1,0:T(8,128)(2,1)}, u32[]{:S(2)}) copy-start(bf16[128,256]{1,0:T(8,128)(2,1)} %constant.68.clone.fh_ref) | copy-start | bytes 196612
  38.8 20.7 %copy-start.1 = (f32[128,128]{1,0:T(8,128)S(1)}, f32[128,128]{1,0:T(8,128)}, u32[]{:S(2)}) copy-start(f32[128,128]{1,0:T(8,128)} %constant.67.clone.wim_ref) | copy-start | bytes 196612
  38.8 20.7 %copy-start.2 = (f32[128,128]{1,0:T(8,128)S(1)}, f32[128,128]{1,0:T(8,128)}, u32[]{:S(2)}) copy-start(f32[128,128]{1,0:T(8,128)} %constant.66.clone.wre_ref) | copy-start | bytes 196612
  38.8 20.7 %copy-start.3 = (bf16[128,256]{1,0:T(8,128)(2,1)S(1)}, bf16[128,256]{1,0:T(8,128)(2,1)}, u32[]{:S(2)}) copy-start(bf16[128,256]{1,0:T(8,128)(2,1)} %constant.65.clone.el_ref) | copy-start | bytes 196612
  38.8 20.7 %copy-start.4 = (bf16[128,256]{1,0:T(8,128)(2,1)S(1)}, bf16[128,256]{1,0:T(8,128)(2,1)}, u32[]{:S(2)}) copy-start(bf16[128,256]{1,0:T(8,128)(2,1)} %constant.64.clone.eh_ref) | copy-start | bytes 196612
  38.8 20.7 %copy-start.5 = (bf16[128,128]{1,0:T(8,128)(2,1)S(1)}, bf16[128,128]{1,0:T(8,128)(2,1)}, u32[]{:S(2)}) copy-start(bf16[128,128]{1,0:T(8,128)(2,1)} %constant.69.clone.fl_ref) | copy-start | bytes 98308

commit v3 on v2

--- a/solution.py
+++ b/solution.py
@@ -108,6 +108,7 @@
     sign = jnp.where(lane < TILE, -1.0, 1.0).astype(jnp.float32)
     span = COARSE * TILE
     pairs = 2
+    shares = fh_ref.shape[0]
 
     @pl.loop(0, STEP // (2 * pairs))
     def _(part):
@@ -129,11 +130,11 @@
                     fh_ref[...], jnp.concatenate([high, low], axis=1), ((1,), (1,))
                 ) + mm(fl_ref[...], high, ((1,), (1,)))
                 turn_ref[
-                    pl.ds(part * (2 * pairs) + pair * 2 + n, 2 * TILE, stride=STEP), :
+                    pl.ds(part * (2 * pairs) + pair * 2 + n, shares, stride=STEP), :
                 ] = result
 
     out_ref[:, pl.ds(pl.multiple_of(line0, STEP), STEP), :] = (
-        turn_ref[...].reshape(2 * TILE, STEP, COARSE).astype(jnp.bfloat16)
+        turn_ref[...].reshape(shares, STEP, COARSE).astype(jnp.bfloat16)
     )
 
 
@@ -152,55 +153,58 @@
     stage_ref, turn_ref, send_sem, recv_sem, own_sem,
 ):
     tables_of = (eh_ref, el_ref, wre_ref, wim_ref, fh_ref, fl_ref)
-    devices = groups * owners
+    near = owners // 2
+    peers = groups * near
     strips = stage_ref.shape[1] // TILE
-    share = stage_ref.shape[0] // devices
-    me = lax.axis_index("grp") * owners + lax.axis_index("dev")
-
-    def piece(strip, peer):
-        rows = pl.ds(strip * TILE, TILE)
+    per_owner = got_ref.shape[2] // TILE
+    share = stage_ref.shape[0] // peers
+    group, place = lax.axis_index("grp"), lax.axis_index("dev")
+    side = place // near
+    mine = group * near + place % near
+
+    def owner_of(peer, strip):
+        at = side if strip < per_owner else 1 - side
+        return (peer // near) * owners + at * near + peer % near
+
+    def piece(strip, peer, source):
         return pltpu.make_async_remote_copy(
-            src_ref=stage_ref.at[pl.ds(peer * share, share), rows, :],
-            dst_ref=got_ref.at[me, :, rows, :],
+            src_ref=stage_ref.at[pl.ds(peer * share, share), pl.ds(strip * TILE, TILE), :],
+            dst_ref=got_ref.at[
+                owner_of(source, strip), :, pl.ds(strip % per_owner * TILE, TILE), :
+            ],
             send_sem=send_sem.at[strip, peer],
-            recv_sem=recv_sem.at[strip, me],
-            device_id=(peer // owners, peer % owners),
+            recv_sem=recv_sem.at[strip, source],
+            device_id=(peer // near, side * near + peer % near),
             device_id_type=pl.DeviceIdType.MESH,
         )
 
-    def arrival(strip, peer):
-        rows = pl.ds(strip * TILE, TILE)
-        return pltpu.make_async_remote_copy(
-            src_ref=stage_ref.at[pl.ds(peer * share, share), rows, :],
-            dst_ref=got_ref.at[peer, :, rows, :],
-            send_sem=send_sem.at[strip, peer],
-            recv_sem=recv_sem.at[strip, peer],
-            device_id=(peer // owners, peer % owners),
-            device_id_type=pl.DeviceIdType.MESH,
-        )
-
-    own = pltpu.make_async_copy(
-        stage_ref.at[pl.ds(me * share, share), :, :], got_ref.at[me], own_sem
-    )
     for strip in range(strips):
         @pl.loop(0, TILE // STEP)
         def _(block):
             transform_block(grid_ref, tables_of, stage_ref, turn_ref, strip * TILE + block * STEP)
 
-        @pl.loop(1, devices)
+        @pl.loop(1, peers)
         def _(n):
-            piece(strip, (me + n) % devices).start()
-
-    own.start()
-    own.wait()
+            piece(strip, (mine + n) % peers, mine).start()
+
+    lines = per_owner * TILE
+    for part in range(2):
+        own = pltpu.make_async_copy(
+            stage_ref.at[pl.ds(mine * share, share), pl.ds(part * lines, lines), :],
+            got_ref.at[owner_of(mine, part * per_owner)],
+            own_sem.at[part],
+        )
+        own.start()
+        own.wait()
     for strip in range(strips):
-        @pl.loop(1, devices)
+        @pl.loop(1, peers)
         def _(n):
-            piece(strip, (me + n) % devices).wait_send()
-
-        @pl.loop(1, devices)
+            piece(strip, (mine + n) % peers, mine).wait_send()
+
+        @pl.loop(1, peers)
         def _(n):
-            arrival(strip, (me + n) % devices).wait_recv()
+            peer = (mine + n) % peers
+            piece(strip, peer, peer).wait_recv()
 
 
 def column_kernel(
@@ -279,11 +283,18 @@
         axis=1,
     )
     sent = mm(place, payload).astype(jnp.bfloat16).reshape(devices, capacity, 3 * VIS)
+    groups, owners = lax.axis_size("grp"), lax.axis_size("dev")
+    copies = 2 if width >= COARSE else 1
+    if copies == 2:
+        other = sent.reshape(groups, 2, owners // 2, capacity, 3 * VIS)[:, ::-1]
+        sent = jnp.concatenate([sent, other.reshape(sent.shape)], axis=1)
     got = lax.all_to_all(sent, AXES, split_axis=0, concat_axis=0, tiled=True)
+    total = copies * total
     got = got.reshape(total, 3 * VIS)
     vis_in = got[:, : 2 * VIS].astype(jnp.float32)
     label_in = got[:, 2 * VIS : 2 * VIS + 5].astype(jnp.int32)
-    tile_in = label_in[:, 0] * COARSE + label_in[:, 1]
+    part = jnp.arange(total, dtype=jnp.int32) // capacity % copies
+    tile_in = (part * (lines // TILE) + label_in[:, 0]) * COARSE + label_in[:, 1]
 
     left = jnp.concatenate([kernels[0], kernels[0]], axis=2)
     right = jnp.swapaxes(kernels[1], 1, 2)
@@ -295,29 +306,39 @@
     vmem = pl.BlockSpec(memory_space=pltpu.VMEM)
     field = pl.pallas_call(
         grid_kernel,
-        out_shape=jax.ShapeDtypeStruct((lines * COARSE, 2 * TILE), jnp.float32),
+        out_shape=jax.ShapeDtypeStruct((copies * lines * COARSE, 2 * TILE), jnp.float32),
         in_specs=[smem] * 4 + [vmem] * 3,
         out_specs=vmem,
-        compiler_params=pltpu.CompilerParams(vmem_limit_bytes=40 << 20),
+        compiler_params=pltpu.CompilerParams(vmem_limit_bytes=48 << 20),
         name="grid_cells",
     )(tile_in, label_in[:, 2], label_in[:, 3], label_in[:, 4], vis_in, left, right)
+    shares = 2 * TILE // copies
+    if copies == 2:
+        side = lax.axis_index("dev") // (owners // 2)
+        row_second = [
+            lax.dynamic_index_in_dim(
+                jnp.asarray(table).reshape(groups, 2, shares // groups, table.shape[1]),
+                side, 1, keepdims=False,
+            ).reshape(shares, table.shape[1])
+            for table in row_second
+        ]
     row_tables = (*row_first, *row_turn, *row_second)
-    turned = pltpu.VMEM((2 * TILE * STEP, COARSE), jnp.float32)
-    if width >= COARSE:
+    turned = pltpu.VMEM((shares * STEP, COARSE), jnp.float32)
+    if copies == 2:
         columns = pl.pallas_call(
-            functools.partial(send_kernel, lax.axis_size("grp"), lax.axis_size("dev")),
+            functools.partial(send_kernel, groups, owners),
             out_shape=jax.ShapeDtypeStruct((devices, 2 * blocks, lines, COARSE), jnp.bfloat16),
             in_specs=[vmem] * 7,
             out_specs=pl.BlockSpec(memory_space=pl.ANY),
             scratch_shapes=[
-                pltpu.VMEM((2 * TILE, lines, COARSE), jnp.bfloat16),
+                pltpu.VMEM((shares, copies * lines, COARSE), jnp.bfloat16),
                 turned,
-                pltpu.SemaphoreType.DMA((lines // TILE, devices)),
-                pltpu.SemaphoreType.DMA((lines // TILE, devices)),
-                pltpu.SemaphoreType.DMA,
+                pltpu.SemaphoreType.DMA((copies * lines // TILE, devices // copies)),
+                pltpu.SemaphoreType.DMA((copies * lines // TILE, devices // copies)),
+                pltpu.SemaphoreType.DMA((2,)),
             ],
             compiler_params=pltpu.CompilerParams(
-                vmem_limit_bytes=52 << 20, has_side_effects=True
+                vmem_limit_bytes=54 << 20, has_side_effects=True
             ),
             name="rows_sent",
         )(field, *row_tables)

time: 347 us -> 353 us (1.017); the launches traced: 346 us -> 347 us
  Pallas kernels: 307 us -> 289 us
  waiting for transfers between devices: 18.7 us -> 35.4 us
    pallas_call x2, Pallas kernels: 249 us -> 231 us  [the longest x1 182 us: local(): pl.pallas_call(functools.partial(send_kernel, groups, owners), out_shape=...]
    all_to_all x1, waiting for transfers between devices: 18.7 us -> 35.4 us  [local(): got = lax.all_to_all(sent, AXES, split_axis=0, concat_axis=0, tiled=True)]
where the time goes in v3:
time: 353 us; the launch traced here: 347 us
  Pallas kernels  289 us (82%)
  waiting for transfers between devices  35.4 us (10%)
  starting transfers between devices  7.41 us (2%)
  other arithmetic  6.8 us (2%)
  local copies, waits for them, and re-layouts  6.48 us (2%)
    pallas_call x1, Pallas kernels, local(): pl.pallas_call(functools.partial(send_kernel, groups, owners), out_shape=...  182 us
    pallas_call x1, Pallas kernels, local(): pl.pallas_call(column_kernel, grid=(blocks,), out_shape=jax.ShapeDtypeStr...  57.8 us
    pallas_call x1, Pallas kernels, local(): pl.pallas_call(grid_kernel, out_shape=jax.ShapeDtypeStruct((copies * line...  49.3 us
    all_to_all x1, waiting for transfers between devices, local(): got = lax.all_to_all(sent, AXES, split_axis=0, concat_axis=0, tiled=True)  35.4 us
    all_to_all x1, starting transfers between devices, local(): got = lax.all_to_all(sent, AXES, split_axis=0, concat_axis=0, tiled=True)  7.41 us
  transfers between devices with their start and end apart: 1, of which 1 were waited for; matrix products, arithmetic and copies ran while one was open for 1% of the time, Pallas kernels for 0%

profile of v3, /device:TPU:0, one launch (start us, length us, event | category | flops | bytes accessed | tf_op | source)
XLA Modules:
  0.0 347.2 jit_solution(4270101889520899394)
XLA Ops:
  0.0 1.0 fusion.5
  1.0 0.7 convert_add_fusion
  1.7 0.7 convert.15
  2.4 0.7 fusion.23
  3.1 0.1 pad.18.clone
  3.2 0.1 maximum_maximum_fusion
  3.3 0.2 copy.25
  3.5 1.0 copy.28
  4.5 0.7 fusion.4
  5.2 0.1 rev.3
  5.3 1.4 pad_maximum_fusion
  6.7 7.4 %all-to-all-start = ((bf16[32,64,384]{2,1,0:T(8,128)(2,1)}), bf16[32,64,384]{2,1,0:T(8,128)(2,1)}, u32[]{:S(2)}, u32[]{:S(2)}) async-start(bf16[32,64,384]{2,1,0:T(8,128)(2,1)} %pad_maximum_fusion), calls=%async_computation | async-start | bytes 3145728 | tf_op jit(solution)/shard_map/all_to_all | solution.py:291
  14.2 0.1 fusion.29
  14.3 1.3 copy.24
  15.6 0.6 constant_dynamic-slice_fusion
  16.2 0.6 constant_dynamic-slice_fusion.1
  16.9 0.6 fusion.2.kb_ref
  17.5 35.4 %all-to-all-done = bf16[32,64,384]{2,1,0:T(8,128)(2,1)} async-done(((bf16[32,64,384]{2,1,0:T(8,128)(2,1)}), bf16[32,64,384]{2,1,0:T(8,128)(2,1)}, u32[]{:S(2)}, u32[]{:S(2)}) %all-to-all-start) | async-done | bytes 1572896 | tf_op jit(solution)/shard_map/all_to_all | solution.py:291
  52.9 1.1 slice_convert_fusion.1
  54.1 1.4 slice_convert_fusion.vis_ref
  55.5 2.5 slice_reduce_fusion
  58.0 49.3 %grid_cells.1.grid_ref = f32[65536,128]{1,0:T(8,128)} custom-call(s32[2048]{0:T(1024)S(1)} %fusion.19.tile_ref, s32[2048]{0:T(1024)S(1)} %get-tuple-element.7.left_ref, s32[2048]{0:T(1024)S(1)} %get-tuple-element.6.right_ref, s32[2048]{0:T(1024)S(1)} %get-tuple-element.5.valid_ref, f32[2048,256]{1,0:T(8,128)S(1)} %slice_convert_fusion.vis_ref, ...), custom_call_target="tpu_custom_call" | custom-call | tf_op jit(solution)/shard_map/grid_cells/pallas_call | solution.py:307
  107.3 182.1 %rows_sent.1 = bf16[32,4,256,128]{3,2,1,0:T(8,128)(2,1)} custom-call(f32[65536,128]{1,0:T(8,128)} %grid_cells.1.grid_ref, bf16[128,256]{1,0:T(8,128)(2,1)} %constant.120.clone.eh_ref, bf16[128,256]{1,0:T(8,128)(2,1)} %constant.121.clone.el_ref, f32[128,128]{1,0:T(8,128)} %constant.122.clone.wre_ref, f32[128,128]{1,0:T(8,128)} %constant.123.clone.wim_ref, ...), custom_call_target="tpu_custom_call" | custom-call | tf_op jit(solution)/shard_map/rows_sent/pallas_call | solution.py:328
  289.4 57.8 %columns.1 = f32[2,256,8192]{2,1,0:T(8,128)} custom-call(bf16[32,2,2,256,128]{4,3,2,1,0:T(8,128)(2,1)} %bitcast.18, bf16[256,256]{1,0:T(8,128)(2,1)} %constant.124.clone.eh_ref, bf16[256,256]{1,0:T(8,128)(2,1)} %constant.125.clone.el_ref, f32[64,128]{1,0:T(8,128)} %constant.126.clone.wre_ref, f32[64,128]{1,0:T(8,128)} %constant.127.clone.wim_ref, ...), custom_call_target="tpu_custom_call" | custom-call | tf_op jit(solution)/shard_map/columns/pallas_call | solution.py:363
  (12 shorter events, 0.1 us)
Async XLA Ops:
  6.7 7.5 %copy-start.1 = (bf16[2,32,64,128]{3,2,1,0:T(8,128)(2,1)S(1)}, bf16[2,32,64,128]{3,2,1,0:T(8,128)(2,1)}, u32[]{:S(2)}) copy-start(bf16[2,32,64,128]{3,2,1,0:T(8,128)(2,1)} %param.21) | copy-start | bytes 3145732
  6.7 46.2 %all-to-all-start = ((bf16[32,64,384]{2,1,0:T(8,128)(2,1)}), bf16[32,64,384]{2,1,0:T(8,128)(2,1)}, u32[]{:S(2)}, u32[]{:S(2)}) async-start(bf16[32,64,384]{2,1,0:T(8,128)(2,1)} %pad_maximum_fusion), calls=%async_computation | async-start | bytes 3145728 | tf_op jit(solution)/shard_map/all_to_all | solution.py:291
  14.1 1.5 copy-start.3
  14.1 2.0 copy-start.2
  15.6 1.3 copy-start

commit v4 on v3

--- a/solution.py
+++ b/solution.py
@@ -44,7 +44,10 @@
     )
     as_real = as_real.reshape(2, TILE // per_device, per_device, 2 * TILE)
     high, low = halves(as_real.transpose(1, 0, 2, 3).reshape(2 * TILE, 2 * TILE))
-    row_second = (np.concatenate([high, high], axis=1), low)
+    row_second = (
+        np.concatenate([high, high], axis=1),
+        np.concatenate([low, np.zeros_like(low)], axis=1),
+    )
     col_first = halves(
         np.concatenate(
             [
@@ -60,7 +63,10 @@
         axis=0,
     )
     high, low = halves(stacked / GRID)
-    col_second = (np.concatenate([high, high], axis=1), low)
+    col_second = (
+        np.concatenate([high, high], axis=1),
+        np.concatenate([low, np.zeros_like(low)], axis=1),
+    )
     return row_first, row_turn, row_second, col_first, col_turn, col_second
 
 
@@ -121,14 +127,18 @@
                 swapped = pltpu.roll(cells, TILE, axis=1) * sign
                 columns.append(jnp.concatenate([cells, swapped], axis=0).astype(jnp.bfloat16))
             both = jnp.concatenate(columns, axis=1)
-            middle = mm(eh_ref[...], both) + mm(el_ref[...], both)
+            middle = mm(jnp.concatenate([eh_ref[...], el_ref[...]], axis=0), both)
+            middle = middle[:COARSE] + middle[COARSE:]
             for n in range(2):
                 value = middle[:, n * 2 * TILE : (n + 1) * 2 * TILE]
                 value = value * wre_ref[...] + pltpu.roll(value, TILE, axis=1) * wim_ref[...]
                 high, low = split(value)
                 result = mm(
-                    fh_ref[...], jnp.concatenate([high, low], axis=1), ((1,), (1,))
-                ) + mm(fl_ref[...], high, ((1,), (1,)))
+                    jnp.concatenate([fh_ref[...], fl_ref[...]], axis=0),
+                    jnp.concatenate([high, low], axis=1),
+                    ((1,), (1,)),
+                )
+                result = result[:shares] + result[shares:]
                 turn_ref[
                     pl.ds(part * (2 * pairs) + pair * 2 + n, shares, stride=STEP), :
                 ] = result
@@ -237,7 +247,11 @@
             at = pl.ds(pl.multiple_of((block * 8 + n) * TILE, TILE), TILE)
             cells = jnp.concatenate([mid_ref[c, at, :] for c in range(2)], axis=0)
             high, low = split(cells)
-            result = mm(fh_ref[...], jnp.concatenate([high, low], axis=0)) + mm(fl_ref[...], high)
+            result = mm(
+                jnp.concatenate([fh_ref[...], fl_ref[...]], axis=0),
+                jnp.concatenate([high, low], axis=0),
+            )
+            result = result[: 2 * TILE] + result[2 * TILE :]
             turn_ref[pl.ds(n, 2 * TILE, stride=8), :] = result
         rows = pl.ds(pl.multiple_of(block * 8, 8), 8)
         for c in range(2):

time: 353 us -> 329 us (0.932); the launches traced: 347 us -> 328 us
  Pallas kernels: 289 us -> 270 us
    pallas_call x1, Pallas kernels: 182 us -> 157 us  [local(): pl.pallas_call(functools.partial(send_kernel, groups, owners), out_shape=...]
    pallas_call x1, Pallas kernels: 49.3 us -> 53.5 us  [local(): pl.pallas_call(grid_kernel, out_shape=jax.ShapeDtypeStruct((copies * line...]
where the time goes in v4:
time: 329 us; the launch traced here: 328 us
  Pallas kernels  270 us (82%)
  waiting for transfers between devices  35.5 us (11%)
  starting transfers between devices  7.41 us (2%)
  other arithmetic  6.8 us (2%)
  local copies, waits for them, and re-layouts  6.45 us (2%)
    pallas_call x1, Pallas kernels, local(): pl.pallas_call(functools.partial(send_kernel, groups, owners), out_shape=...  157 us
    pallas_call x1, Pallas kernels, local(): pl.pallas_call(column_kernel, grid=(blocks,), out_shape=jax.ShapeDtypeStr...  59.7 us
    pallas_call x1, Pallas kernels, local(): pl.pallas_call(grid_kernel, out_shape=jax.ShapeDtypeStruct((copies * line...  53.5 us
    all_to_all x1, waiting for transfers between devices, local(): got = lax.all_to_all(sent, AXES, split_axis=0, concat_axis=0, tiled=True)  35.5 us
    all_to_all x1, starting transfers between devices, local(): got = lax.all_to_all(sent, AXES, split_axis=0, concat_axis=0, tiled=True)  7.41 us
  transfers between devices with their start and end apart: 1, of which 1 were waited for; matrix products, arithmetic and copies ran while one was open for 1% of the time, Pallas kernels for 0%

profile of v4, /device:TPU:0, one launch (start us, length us, event | category | flops | bytes accessed | tf_op | source)
XLA Modules:
  0.0 328.0 jit_solution(11364476453997490404)
XLA Ops:
  0.0 1.0 fusion.5
  1.0 0.7 convert_add_fusion
  1.7 0.7 convert.15
  2.4 0.7 fusion.23
  3.1 0.1 pad.18.clone
  3.2 0.1 maximum_maximum_fusion
  3.3 0.2 copy.25
  3.5 1.0 copy.28
  4.5 0.7 fusion.4
  5.2 0.1 rev.3
  5.3 1.4 pad_maximum_fusion
  6.7 7.4 %all-to-all-start = ((bf16[32,64,384]{2,1,0:T(8,128)(2,1)}), bf16[32,64,384]{2,1,0:T(8,128)(2,1)}, u32[]{:S(2)}, u32[]{:S(2)}) async-start(bf16[32,64,384]{2,1,0:T(8,128)(2,1)} %pad_maximum_fusion), calls=%async_computation | async-start | bytes 3145728 | tf_op jit(solution)/shard_map/all_to_all | solution.py:305
  14.2 0.1 fusion.29
  14.3 1.3 copy.24
  15.6 0.6 constant_dynamic-slice_fusion
  16.3 0.5 copy-done
  16.8 0.6 fusion.2.kb_ref
  17.5 35.5 %all-to-all-done = bf16[32,64,384]{2,1,0:T(8,128)(2,1)} async-done(((bf16[32,64,384]{2,1,0:T(8,128)(2,1)}), bf16[32,64,384]{2,1,0:T(8,128)(2,1)}, u32[]{:S(2)}, u32[]{:S(2)}) %all-to-all-start) | async-done | bytes 1572896 | tf_op jit(solution)/shard_map/all_to_all | solution.py:305
  52.9 1.1 slice_convert_fusion.1
  54.1 1.4 slice_convert_fusion.vis_ref
  55.5 2.5 slice_reduce_fusion
  58.0 53.5 %grid_cells.1.grid_ref = f32[65536,128]{1,0:T(8,128)} custom-call(s32[2048]{0:T(1024)S(1)} %fusion.19.tile_ref, s32[2048]{0:T(1024)S(1)} %get-tuple-element.7.left_ref, s32[2048]{0:T(1024)S(1)} %get-tuple-element.6.right_ref, s32[2048]{0:T(1024)S(1)} %get-tuple-element.5.valid_ref, f32[2048,256]{1,0:T(8,128)S(1)} %slice_convert_fusion.vis_ref, ...), custom_call_target="tpu_custom_call" | custom-call | tf_op jit(solution)/shard_map/grid_cells/pallas_call | solution.py:321
  111.6 156.7 %rows_sent.1 = bf16[32,4,256,128]{3,2,1,0:T(8,128)(2,1)} custom-call(f32[65536,128]{1,0:T(8,128)} %grid_cells.1.grid_ref, bf16[128,256]{1,0:T(8,128)(2,1)} %constant.118.clone.eh_ref, bf16[128,256]{1,0:T(8,128)(2,1)} %constant.119.clone.el_ref, f32[128,128]{1,0:T(8,128)} %constant.120.clone.wre_ref, f32[128,128]{1,0:T(8,128)} %constant.121.clone.wim_ref, ...), custom_call_target="tpu_custom_call" | custom-call | tf_op jit(solution)/shard_map/rows_sent/pallas_call | solution.py:342
  268.3 59.7 %columns.1 = f32[2,256,8192]{2,1,0:T(8,128)} custom-call(bf16[32,2,2,256,128]{4,3,2,1,0:T(8,128)(2,1)} %bitcast.18, bf16[256,256]{1,0:T(8,128)(2,1)} %constant.122.clone.eh_ref, bf16[256,256]{1,0:T(8,128)(2,1)} %constant.123.clone.el_ref, f32[64,128]{1,0:T(8,128)} %constant.124.clone.wre_ref, f32[64,128]{1,0:T(8,128)} %constant.125.clone.wim_ref, ...), custom_call_target="tpu_custom_call" | custom-call | tf_op jit(solution)/shard_map/columns/pallas_call | solution.py:377
  (11 shorter events, 0.1 us)
Async XLA Ops:
  6.7 7.5 %copy-start.1 = (bf16[2,32,64,128]{3,2,1,0:T(8,128)(2,1)S(1)}, bf16[2,32,64,128]{3,2,1,0:T(8,128)(2,1)}, u32[]{:S(2)}) copy-start(bf16[2,32,64,128]{3,2,1,0:T(8,128)(2,1)} %param.21) | copy-start | bytes 3145732
  6.7 46.2 %all-to-all-start = ((bf16[32,64,384]{2,1,0:T(8,128)(2,1)}), bf16[32,64,384]{2,1,0:T(8,128)(2,1)}, u32[]{:S(2)}, u32[]{:S(2)}) async-start(bf16[32,64,384]{2,1,0:T(8,128)(2,1)} %pad_maximum_fusion), calls=%async_computation | async-start | bytes 3145728 | tf_op jit(solution)/shard_map/all_to_all | solution.py:305
  14.1 1.5 copy-start.2
  14.1 1.4 copy-start.3
  15.6 1.2 copy-start
